TPU v7x, 512 devices: a whole 4x8x8 slice. The times are simulated.
512 devices in a mesh: row: 64 (over x, z, core), col: 8 (over y).
Axes of the slice: x: 4, y: 8, z: 8, core: 2. Of those that a mesh axis runs over, the one named last changes fastest.
Arguments:
- trailing: float32 [32768, 8192], P('row', 'col'), may hold values from -6 to 6
- reflectors: float32 [32768, 256], P('row', 'col'), may hold values from -0.25 to 0.25
- leaf_factor: float32 [16384, 256], P('row', 'col'), may hold values from -0.5 to 0.5
- node_reflect: float32 [6, 16384, 256], P(None, 'row', 'col'), may hold values from -0.375 to 0.375
- node_factor: float32 [6, 16384, 256], P(None, 'row', 'col'), may hold values from -0.5 to 0.5
Outputs:
- updated: float32 [32768, 8192], P('row', 'col')
All inputs are finite; a program needn't handle non-finite values.
Results may differ from a plain program's by a relative error of at most 0.00014.
Values sent between devices are 32-bit elements; how exact they have to be, the bound alone decides.
A program may use at most 64 MiB of HBM per device.

v0:
```python
import jax
import jax.numpy as jnp
from jax import lax
from jax.sharding import PartitionSpec as P

B = 256
highest = lax.Precision.HIGHEST


def turned_gather(arrays, axis, dims):
    turned = [jnp.moveaxis(a, dim, 0) for a, dim in zip(arrays, dims)]
    both = jnp.concatenate([t.reshape(len(t), -1) for t in turned], axis=1)
    whole, at, done = (lax.all_gather(both, axis, axis=0, tiled=True), 0, [])
    for t, dim in zip(turned, dims):
        section = whole[:, at : at + t[0].size].reshape(-1, *t.shape[1:])
        done.append(jnp.moveaxis(section, 0, dim))
        at += t[0].size
    return tuple(done)


def swapped(value, axis, apart):
    mask = 2**apart
    pairs = [(source, source ^ mask) for source in range(lax.axis_size(axis))]
    return lax.ppermute(value, axis, pairs)


def triangle(factor):
    return jnp.triu(factor) + 0.5 * jnp.eye(factor.shape[-1], dtype=factor.dtype)


def combine(upper_rows, partner_rows, other_piece, node_y, node_full, clear):
    chosen_y = jnp.where(clear, other_piece, node_y)
    chosen_tri = triangle(jnp.where(clear, node_full, other_piece))
    leader_rows = jnp.where(clear, upper_rows, partner_rows)
    follower_rows = jnp.where(clear, partner_rows, upper_rows)
    summed = leader_rows + jnp.einsum("kb,kc->bc", chosen_y, follower_rows, precision=highest)
    coupling = jnp.einsum("kb,kc->bc", chosen_tri, summed, precision=highest)
    lowered = upper_rows - jnp.einsum("bk,kc->bc", chosen_y, coupling, precision=highest)
    return jnp.where(clear, upper_rows - coupling, lowered)


def per_device(trailing, reflectors, leaf_factor, node_reflect, node_factor):
    vectors, leaf_full, node_y_all, node_f_all = turned_gather(
        (reflectors, leaf_factor, node_reflect, node_factor), "col", (1, 1, 2, 2)
    )
    leaf_tri = triangle(leaf_full)
    inner = jnp.einsum("rb,rc->bc", vectors, trailing, precision=highest)
    scaled = jnp.einsum("kb,kc->bc", leaf_tri, inner, precision=highest)
    leafed = trailing - jnp.einsum("rb,bc->rc", vectors, scaled, precision=highest)
    upper_rows = leafed[:B]
    remainder = leafed[B:]
    position = lax.axis_index("row")
    levels = lax.axis_size("row").bit_length() - 1
    clears = []
    pieces = []
    for section in range(levels):
        clear = position // (1 << section) % 2 == 0
        clears.append(clear)
        pieces.append(jnp.where(clear, node_f_all[section], node_y_all[section]))
    for section in range(levels):
        partner_rows, other_piece = swapped((upper_rows, pieces[section]), "row", section)
        upper_rows = combine(
            upper_rows,
            partner_rows,
            other_piece,
            node_y_all[section],
            node_f_all[section],
            clears[section],
        )
    return jnp.concatenate([upper_rows, remainder], axis=0)


def solution(mesh):
    in_specs = (
        P("row", "col"),
        P("row", "col"),
        P("row", "col"),
        P(None, "row", "col"),
        P(None, "row", "col"),
    )
    out_specs = P("row", "col")
    return jax.shard_map(
        per_device, mesh=mesh, in_specs=in_specs, out_specs=out_specs, check_vma=False
    )
```

profile of v0, /device:TPU:2, one launch (start us, length us, event | category | flops | bytes accessed | tf_op | source)
XLA Modules:
  0.0 353.9 jit_solution(16999531259912984661)
XLA Ops:
  6.5 0.0 all-gather.2.cloned.1.call-start
  6.5 1.1 copy.14
  7.6 0.9 copy.15
  8.6 1.7 pad_maximum_fusion.1
  10.3 0.0 all-gather.2.cloned.1.call-update
  10.4 59.3 %all-gather.2.cloned.1.call-done = f32[256,3840]{1,0:T(8,128)} async-done(((f32[32,3840]{1,0:T(8,128)}), f32[256,3840]{1,0:T(8,128)}) %all-gather.2.cloned.1.call-update) | async-done | bytes 3932176 | tf_op jit(solution)/shard_map/all_gather | solution.py:13
  69.7 0.0 copy-done.2
  69.7 3.1 fusion.43
  72.8 0.0 copy-start.3
  72.8 2.1 fusion.45
  74.9 0.0 copy-done.4
  74.9 0.0 copy-done.3
  75.0 1.9 convolution_subtract_fusion
  76.9 1.2 fusion.140
  78.1 1.9 collective-permute-start.1
  80.0 2.1 fusion.139
  82.1 3.0 copy.12
  85.2 3.0 copy.13
  88.2 3.0 copy.10
  91.2 3.0 copy.11
  94.3 2.1 fusion.70
  96.4 2.5 collective-permute-start
  99.0 1.1 collective-permute-done
  100.1 0.0 collective-permute-done.1
  100.1 2.3 fusion.27
  102.4 0.0 copy-done.1
  102.4 1.2 fusion.25
  103.6 1.2 subtract_select_fusion.5
  104.8 3.6 %collective-permute-start.3 = (f32[256,1024]{1,0:T(8,128)S(1)}, f32[256,1024]{1,0:T(8,128)S(1)}, u32[]{:S(2)}, u32[]{:S(2)}) collective-permute-start(f32[256,1024]{1,0:T(8,128)S(1)} %subtract_select_fusion.5), channel_id=1, source_target_pairs={{0,16},{8,24},{16,0},{24,8},{32,48},{40,56},{48,32},{56,40},{64,80... | collective-permute-start | bytes 3145736 | tf_op jit(solution)/shard_map/ppermute | solution.py:24
  108.3 2.5 collective-permute-start.2
  110.8 26.9 %collective-permute-done.2 = f32[256,256]{0,1:T(8,128)S(1)} collective-permute-done((f32[256,256]{0,1:T(8,128)S(1)}, f32[256,256]{0,1:T(8,128)S(1)}, u32[]{:S(2)}, u32[]{:S(2)}) %collective-permute-start.2) | collective-permute-done | bytes 262176 | tf_op jit(solution)/shard_map/ppermute | solution.py:24
  137.7 0.0 collective-permute-done.3
  137.7 1.1 fusion.22
  138.8 1.2 fusion.20
  140.0 1.2 subtract_select_fusion.4
  141.2 4.6 %collective-permute-start.5 = (f32[256,1024]{1,0:T(8,128)S(1)}, f32[256,1024]{1,0:T(8,128)S(1)}, u32[]{:S(2)}, u32[]{:S(2)}) collective-permute-start(f32[256,1024]{1,0:T(8,128)S(1)} %subtract_select_fusion.4), channel_id=1, source_target_pairs={{0,32},{8,40},{16,48},{24,56},{32,0},{40,8},{48,16},{56,24},{64,96... | collective-permute-start | bytes 3145736 | tf_op jit(solution)/shard_map/ppermute | solution.py:24
  145.8 2.1 collective-permute-start.4
  147.9 54.4 %collective-permute-done.4 = f32[256,256]{0,1:T(8,128)S(1)} collective-permute-done((f32[256,256]{0,1:T(8,128)S(1)}, f32[256,256]{0,1:T(8,128)S(1)}, u32[]{:S(2)}, u32[]{:S(2)}) %collective-permute-start.4) | collective-permute-done | bytes 262176 | tf_op jit(solution)/shard_map/ppermute | solution.py:24
  202.3 0.0 collective-permute-done.5
  202.3 1.1 fusion.17
  203.4 1.2 fusion.15
  204.6 1.2 subtract_select_fusion.3
  205.8 7.9 %collective-permute-start.7 = (f32[256,1024]{1,0:T(8,128)S(1)}, f32[256,1024]{1,0:T(8,128)S(1)}, u32[]{:S(2)}, u32[]{:S(2)}) collective-permute-start(f32[256,1024]{1,0:T(8,128)S(1)} %subtract_select_fusion.3), channel_id=1, source_target_pairs={{0,64},{8,72},{16,80},{24,88},{32,96},{40,104},{48,112},{56,120},{... | collective-permute-start | bytes 3145736 | tf_op jit(solution)/shard_map/ppermute | solution.py:24
  213.7 1.9 collective-permute-start.6
  215.6 55.4 %collective-permute-done.6 = f32[256,256]{0,1:T(8,128)S(1)} collective-permute-done((f32[256,256]{0,1:T(8,128)S(1)}, f32[256,256]{0,1:T(8,128)S(1)}, u32[]{:S(2)}, u32[]{:S(2)}) %collective-permute-start.6) | collective-permute-done | bytes 262176 | tf_op jit(solution)/shard_map/ppermute | solution.py:24
  271.0 0.0 collective-permute-done.7
  271.0 1.1 fusion.12
  272.1 1.2 fusion.10
  273.3 1.2 subtract_select_fusion.2
  274.5 2.5 collective-permute-start.9
  276.9 3.6 %collective-permute-start.8 = (f32[256,256]{0,1:T(8,128)S(1)}, f32[256,256]{0,1:T(8,128)S(1)}, u32[]{:S(2)}, u32[]{:S(2)}) collective-permute-start(f32[256,256]{0,1:T(8,128)S(1)} %get-tuple-element.8), channel_id=1, source_target_pairs={{0,128},{8,136},{16,144},{24,152},{32,160},{40,168},{48,176},{56,1... | collective-permute-start | bytes 786440 | tf_op jit(solution)/shard_map/ppermute | solution.py:24
  280.5 25.7 %collective-permute-done.8 = f32[256,256]{0,1:T(8,128)S(1)} collective-permute-done((f32[256,256]{0,1:T(8,128)S(1)}, f32[256,256]{0,1:T(8,128)S(1)}, u32[]{:S(2)}, u32[]{:S(2)}) %collective-permute-start.8) | collective-permute-done | bytes 262176 | tf_op jit(solution)/shard_map/ppermute | solution.py:24
  306.2 0.0 collective-permute-done.9
  306.2 1.1 fusion.7
  307.3 1.2 fusion.5
  308.5 1.2 subtract_select_fusion.1
  309.7 4.0 %collective-permute-start.11 = (f32[256,1024]{1,0:T(8,128)S(1)}, f32[256,1024]{1,0:T(8,128)S(1)}, u32[]{:S(2)}, u32[]{:S(2)}) collective-permute-start(f32[256,1024]{1,0:T(8,128)S(1)} %subtract_select_fusion.1), channel_id=1, source_target_pairs={{0,256},{8,264},{16,272},{24,280},{32,288},{40,296},{48,304},{56,3... | collective-permute-start | bytes 3145736 | tf_op jit(solution)/shard_map/ppermute | solution.py:24
  313.7 3.4 collective-permute-start.10
  317.0 25.1 %collective-permute-done.10 = f32[256,256]{0,1:T(8,128)S(1)} collective-permute-done((f32[256,256]{0,1:T(8,128)S(1)}, f32[256,256]{0,1:T(8,128)S(1)}, u32[]{:S(2)}, u32[]{:S(2)}) %collective-permute-start.10) | collective-permute-done | bytes 262176 | tf_op jit(solution)/shard_map/ppermute | solution.py:24
  342.1 0.0 collective-permute-done.11
  342.1 1.1 fusion.2
  343.2 1.2 fusion
  344.4 1.2 subtract_select_fusion
  345.6 1.5 pad_maximum_fusion
  (6 shorter events, 0.0 us)
Async XLA Ops:
  6.5 63.1 %copy-start.2 = (f32[512,1024]{1,0:T(8,128)S(1)}, f32[512,1024]{1,0:T(8,128)}, u32[]{:S(2)}) copy-start(f32[512,1024]{1,0:T(8,128)} %param.5) | copy-start | bytes 6291460
  6.5 63.1 %all-gather.2.cloned.1.call-start = ((), (), s32[]{:S(2)}) async-start(), calls=%async_computation | async-start | bytes 4423680 | tf_op jit(solution)/shard_map/all_gather | solution.py:13
  69.7 5.3 %copy-start.4 = (f32[256,3840]{1,0:T(8,128)S(1)}, f32[256,3840]{1,0:T(8,128)}, u32[]{:S(2)}) copy-start(f32[256,3840]{1,0:T(8,128)} %all-gather.2.cloned.1.call-done) | copy-start | bytes 11796484
  72.8 2.2 copy-start.3
  78.1 22.0 %collective-permute-start.1 = (f32[256,1024]{1,0:T(8,128)}, f32[256,1024]{1,0:T(8,128)}, u32[]{:S(2)}, u32[]{:S(2)}) collective-permute-start(f32[256,1024]{1,0:T(8,128)} %get-tuple-element.13), channel_id=1, source_target_pairs={{0,8},{8,0},{16,24},{24,16},{32,40},{40,32},{48,56},{56,48},{64,72... | collective-permute-start | bytes 3145736 | tf_op jit(solution)/shard_map/ppermute | solution.py:24
  94.3 5.8 %copy-start = (f32[256,6,256]{2,0,1:T(8,128)S(1)}, f32[256,6,256]{2,0,1:T(8,128)}, u32[]{:S(2)}) copy-start(f32[256,6,256]{2,0,1:T(8,128)} %copy.13) | copy-start | bytes 4718596
  96.4 6.0 %copy-start.1 = (f32[256,6,256]{2,0,1:T(8,128)S(1)}, f32[256,6,256]{2,0,1:T(8,128)}, u32[]{:S(2)}) copy-start(f32[256,6,256]{2,0,1:T(8,128)} %copy.11) | copy-start | bytes 4718596
  96.4 3.7 %collective-permute-start = (f32[256,256]{0,1:T(8,128)S(1)}, f32[256,256]{0,1:T(8,128)S(1)}, u32[]{:S(2)}, u32[]{:S(2)}) collective-permute-start(f32[256,256]{0,1:T(8,128)S(1)} %get-tuple-element.12), channel_id=1, source_target_pairs={{0,8},{8,0},{16,24},{24,16},{32,40},{40,32},{48,56},{56,48},{64,72... | collective-permute-start | bytes 786440 | tf_op jit(solution)/shard_map/ppermute | solution.py:24
  104.8 32.9 %collective-permute-start.3 = (f32[256,1024]{1,0:T(8,128)S(1)}, f32[256,1024]{1,0:T(8,128)S(1)}, u32[]{:S(2)}, u32[]{:S(2)}) collective-permute-start(f32[256,1024]{1,0:T(8,128)S(1)} %subtract_select_fusion.5), channel_id=1, source_target_pairs={{0,16},{8,24},{16,0},{24,8},{32,48},{40,56},{48,32},{56,40},{64,80... | collective-permute-start | bytes 3145736 | tf_op jit(solution)/shard_map/ppermute | solution.py:24
  108.3 29.4 %collective-permute-start.2 = (f32[256,256]{0,1:T(8,128)S(1)}, f32[256,256]{0,1:T(8,128)S(1)}, u32[]{:S(2)}, u32[]{:S(2)}) collective-permute-start(f32[256,256]{0,1:T(8,128)S(1)} %get-tuple-element.11), channel_id=1, source_target_pairs={{0,16},{8,24},{16,0},{24,8},{32,48},{40,56},{48,32},{56,40},{64,80... | collective-permute-start | bytes 786440 | tf_op jit(solution)/shard_map/ppermute | solution.py:24
  141.2 61.2 %collective-permute-start.5 = (f32[256,1024]{1,0:T(8,128)S(1)}, f32[256,1024]{1,0:T(8,128)S(1)}, u32[]{:S(2)}, u32[]{:S(2)}) collective-permute-start(f32[256,1024]{1,0:T(8,128)S(1)} %subtract_select_fusion.4), channel_id=1, source_target_pairs={{0,32},{8,40},{16,48},{24,56},{32,0},{40,8},{48,16},{56,24},{64,96... | collective-permute-start | bytes 3145736 | tf_op jit(solution)/shard_map/ppermute | solution.py:24
  145.8 56.5 %collective-permute-start.4 = (f32[256,256]{0,1:T(8,128)S(1)}, f32[256,256]{0,1:T(8,128)S(1)}, u32[]{:S(2)}, u32[]{:S(2)}) collective-permute-start(f32[256,256]{0,1:T(8,128)S(1)} %get-tuple-element.10), channel_id=1, source_target_pairs={{0,32},{8,40},{16,48},{24,56},{32,0},{40,8},{48,16},{56,24},{64,96... | collective-permute-start | bytes 786440 | tf_op jit(solution)/shard_map/ppermute | solution.py:24
  205.8 65.2 %collective-permute-start.7 = (f32[256,1024]{1,0:T(8,128)S(1)}, f32[256,1024]{1,0:T(8,128)S(1)}, u32[]{:S(2)}, u32[]{:S(2)}) collective-permute-start(f32[256,1024]{1,0:T(8,128)S(1)} %subtract_select_fusion.3), channel_id=1, source_target_pairs={{0,64},{8,72},{16,80},{24,88},{32,96},{40,104},{48,112},{56,120},{... | collective-permute-start | bytes 3145736 | tf_op jit(solution)/shard_map/ppermute | solution.py:24
  213.7 57.3 %collective-permute-start.6 = (f32[256,256]{0,1:T(8,128)S(1)}, f32[256,256]{0,1:T(8,128)S(1)}, u32[]{:S(2)}, u32[]{:S(2)}) collective-permute-start(f32[256,256]{0,1:T(8,128)S(1)} %get-tuple-element.9), channel_id=1, source_target_pairs={{0,64},{8,72},{16,80},{24,88},{32,96},{40,104},{48,112},{56,120},{... | collective-permute-start | bytes 786440 | tf_op jit(solution)/shard_map/ppermute | solution.py:24
  274.5 31.8 %collective-permute-start.9 = (f32[256,1024]{1,0:T(8,128)S(1)}, f32[256,1024]{1,0:T(8,128)S(1)}, u32[]{:S(2)}, u32[]{:S(2)}) collective-permute-start(f32[256,1024]{1,0:T(8,128)S(1)} %subtract_select_fusion.2), channel_id=1, source_target_pairs={{0,128},{8,136},{16,144},{24,152},{32,160},{40,168},{48,176},{56,1... | collective-permute-start | bytes 3145736 | tf_op jit(solution)/shard_map/ppermute | solution.py:24
  276.9 29.3 %collective-permute-start.8 = (f32[256,256]{0,1:T(8,128)S(1)}, f32[256,256]{0,1:T(8,128)S(1)}, u32[]{:S(2)}, u32[]{:S(2)}) collective-permute-start(f32[256,256]{0,1:T(8,128)S(1)} %get-tuple-element.8), channel_id=1, source_target_pairs={{0,128},{8,136},{16,144},{24,152},{32,160},{40,168},{48,176},{56,1... | collective-permute-start | bytes 786440 | tf_op jit(solution)/shard_map/ppermute | solution.py:24
  309.7 32.4 %collective-permute-start.11 = (f32[256,1024]{1,0:T(8,128)S(1)}, f32[256,1024]{1,0:T(8,128)S(1)}, u32[]{:S(2)}, u32[]{:S(2)}) collective-permute-start(f32[256,1024]{1,0:T(8,128)S(1)} %subtract_select_fusion.1), channel_id=1, source_target_pairs={{0,256},{8,264},{16,272},{24,280},{32,288},{40,296},{48,304},{56,3... | collective-permute-start | bytes 3145736 | tf_op jit(solution)/shard_map/ppermute | solution.py:24
  313.7 28.4 %collective-permute-start.10 = (f32[256,256]{0,1:T(8,128)S(1)}, f32[256,256]{0,1:T(8,128)S(1)}, u32[]{:S(2)}, u32[]{:S(2)}) collective-permute-start(f32[256,256]{0,1:T(8,128)S(1)} %get-tuple-element.7), channel_id=1, source_target_pairs={{0,256},{8,264},{16,272},{24,280},{32,288},{40,296},{48,304},{56,3... | collective-permute-start | bytes 786440 | tf_op jit(solution)/shard_map/ppermute | solution.py:24
Sparse Core Ops, SparseCore 0:
  10.4 59.2 all-gather.1
where the time goes:
time: 355 us; the launch traced here: 354 us
  waiting for transfers between devices  248 us (70%)
  starting transfers between devices  40.5 us (11%)
  matrix products  28.9 us (8%)
  local copies, waits for them, and re-layouts  17.5 us (5%)
  between operations  13.8 us (4%)
  other arithmetic  5.28 us (1%)
    ppermute x12, waiting for transfers between devices, swapped(): return lax.ppermute(value, axis, pairs)  189 us
    all_gather x1, waiting for transfers between devices, turned_gather(): whole, at, done = (lax.all_gather(both, axis, axis=0, tiled=True), 0, [])  59.3 us
    ppermute x12, starting transfers between devices, swapped(): return lax.ppermute(value, axis, pairs)  40.5 us
    slice x3, local copies, waits for them, and re-layouts, turned_gather(): section = whole[:, at:at + t[0].size].reshape(-1, *t.shape[1:])  8.18 us
    dot_general x6, matrix products, combine(): jnp.einsum('kb,kc->bc', chosen_y, follower_rows, precision=highest)  7.63 us
    dot_general x6, matrix products, combine(): jnp.einsum('bk,kc->bc', chosen_y, coupling, precision=highest)  7.1 us
  transfers between devices with their start and end apart: 13, of which 7 were waited for; matrix products, arithmetic and copies ran while one was open for 5% of the time, Pallas kernels for 0%

commit v1 on v0

--- a/solution.py
+++ b/solution.py
@@ -10,7 +10,19 @@
 def turned_gather(arrays, axis, dims):
     turned = [jnp.moveaxis(a, dim, 0) for a, dim in zip(arrays, dims)]
     both = jnp.concatenate([t.reshape(len(t), -1) for t in turned], axis=1)
-    whole, at, done = (lax.all_gather(both, axis, axis=0, tiled=True), 0, [])
+    whole, at, done = (
+        jnp.concatenate(
+            lax.all_to_all(
+                jnp.stack([both for _ in range(lax.psum(1, axis_name=axis))]),
+                concat_axis=0,
+                split_axis=0,
+                axis_name=axis,
+            ),
+            axis=0,
+        ),
+        0,
+        [],
+    )
     for t, dim in zip(turned, dims):
         section = whole[:, at : at + t[0].size].reshape(-1, *t.shape[1:])
         done.append(jnp.moveaxis(section, 0, dim))

time: 355 us -> 384 us (1.082)
  the two profiles are of different devices: /device:TPU:2 before, /device:TPU:198 now
where the time goes in v1:
time: 384 us
  waiting for transfers between devices  280 us (73%)
  starting transfers between devices  48 us (12%)
  matrix products  29.8 us (8%)
  local copies, waits for them, and re-layouts  21.1 us (5%)
  other arithmetic  4.5 us (1%)
    ppermute x12, waiting for transfers between devices, swapped(): return lax.ppermute(value, axis, pairs)  189 us
    all_to_all x1, waiting for transfers between devices, turned_gather(): lax.all_to_all(jnp.stack([both for _ in range(lax.psum(1, axis_name=axis)...  90.8 us
    ppermute x12, starting transfers between devices, swapped(): return lax.ppermute(value, axis, pairs)  40.7 us
    slice x3, local copies, waits for them, and re-layouts, turned_gather(): section = whole[:, at:at + t[0].size].reshape(-1, *t.shape[1:])  9.83 us
  transfers between devices with their start and end apart: 13, of which 7 were waited for; matrix products, arithmetic and copies ran while one was open for 5% of the time, Pallas kernels for 0%

profile of v1, /device:TPU:198, one launch (start us, length us, event | category | flops | bytes accessed | tf_op | source)
XLA Modules:
  0.0 383.6 jit_solution(6422449871551888724)
XLA Ops:
  0.0 0.9 copy.17
  0.9 0.9 copy.18
  1.9 0.9 pad_maximum_fusion.1
  2.8 2.2 stack.2
  5.0 7.2 %all-to-all-start = ((f32[8,32,3840]{2,1,0:T(8,128)}), f32[8,32,3840]{2,1,0:T(8,128)}, u32[]{:S(2)}, u32[]{:S(2)}) async-start(f32[8,32,3840]{2,1,0:T(8,128)} %stack.2), calls=%async_computation | async-start | bytes 7864320 | tf_op jit(solution)/shard_map/all_to_all | solution.py:15
  12.2 90.8 %all-to-all-done = f32[8,32,3840]{2,1,0:T(8,128)} async-done(((f32[8,32,3840]{2,1,0:T(8,128)}), f32[8,32,3840]{2,1,0:T(8,128)}, u32[]{:S(2)}, u32[]{:S(2)}) %all-to-all-start) | async-done | bytes 3932192 | tf_op jit(solution)/shard_map/all_to_all | solution.py:15
  103.0 0.0 copy-done.2
  103.0 2.9 fusion.43
  105.9 0.0 copy-start.3
  105.9 2.1 fusion.45
  108.1 0.0 copy-done.3
  108.1 3.0 convolution_subtract_fusion
  111.1 1.2 fusion.140
  112.2 1.9 collective-permute-start.1
  114.1 3.8 fusion.139
  117.9 3.0 copy.15
  121.0 3.1 copy.16
  124.0 3.0 copy.13
  127.0 3.0 copy.14
  130.0 2.1 fusion.70
  132.2 0.0 copy-start.1
  132.2 2.5 collective-permute-start
  134.7 1.1 collective-permute-done
  135.9 0.0 collective-permute-done.1
  135.9 0.0 copy-done
  135.9 2.3 fusion.27
  138.2 1.2 fusion.25
  139.4 1.2 subtract_select_fusion.5
  140.5 1.9 collective-permute-start.3
  142.5 4.1 %collective-permute-start.2 = (f32[256,256]{0,1:T(8,128)S(1)}, f32[256,256]{0,1:T(8,128)S(1)}, u32[]{:S(2)}, u32[]{:S(2)}) collective-permute-start(f32[256,256]{0,1:T(8,128)S(1)} %get-tuple-element.11), channel_id=1, source_target_pairs={{0,16},{8,24},{16,0},{24,8},{32,48},{40,56},{48,32},{56,40},{64,80... | collective-permute-start | bytes 786440 | tf_op jit(solution)/shard_map/ppermute | solution.py:36
  146.6 26.9 %collective-permute-done.2 = f32[256,256]{0,1:T(8,128)S(1)} collective-permute-done((f32[256,256]{0,1:T(8,128)S(1)}, f32[256,256]{0,1:T(8,128)S(1)}, u32[]{:S(2)}, u32[]{:S(2)}) %collective-permute-start.2) | collective-permute-done | bytes 262176 | tf_op jit(solution)/shard_map/ppermute | solution.py:36
  173.5 0.0 collective-permute-done.3
  173.5 1.1 fusion.22
  174.6 1.2 fusion.20
  175.8 1.2 subtract_select_fusion.4
  176.9 1.9 collective-permute-start.5
  178.9 4.8 %collective-permute-start.4 = (f32[256,256]{0,1:T(8,128)S(1)}, f32[256,256]{0,1:T(8,128)S(1)}, u32[]{:S(2)}, u32[]{:S(2)}) collective-permute-start(f32[256,256]{0,1:T(8,128)S(1)} %get-tuple-element.10), channel_id=1, source_target_pairs={{0,32},{8,40},{16,48},{24,56},{32,0},{40,8},{48,16},{56,24},{64,96... | collective-permute-start | bytes 786440 | tf_op jit(solution)/shard_map/ppermute | solution.py:36
  183.7 54.3 %collective-permute-done.4 = f32[256,256]{0,1:T(8,128)S(1)} collective-permute-done((f32[256,256]{0,1:T(8,128)S(1)}, f32[256,256]{0,1:T(8,128)S(1)}, u32[]{:S(2)}, u32[]{:S(2)}) %collective-permute-start.4) | collective-permute-done | bytes 262176 | tf_op jit(solution)/shard_map/ppermute | solution.py:36
  238.0 0.0 collective-permute-done.5
  238.0 1.1 fusion.17
  239.1 1.2 fusion.15
  240.3 1.2 subtract_select_fusion.3
  241.5 8.2 %collective-permute-start.7 = (f32[256,1024]{1,0:T(8,128)S(1)}, f32[256,1024]{1,0:T(8,128)S(1)}, u32[]{:S(2)}, u32[]{:S(2)}) collective-permute-start(f32[256,1024]{1,0:T(8,128)S(1)} %subtract_select_fusion.3), channel_id=1, source_target_pairs={{0,64},{8,72},{16,80},{24,88},{32,96},{40,104},{48,112},{56,120},{... | collective-permute-start | bytes 3145736 | tf_op jit(solution)/shard_map/ppermute | solution.py:36
  249.7 1.9 collective-permute-start.6
  251.6 55.6 %collective-permute-done.6 = f32[256,256]{0,1:T(8,128)S(1)} collective-permute-done((f32[256,256]{0,1:T(8,128)S(1)}, f32[256,256]{0,1:T(8,128)S(1)}, u32[]{:S(2)}, u32[]{:S(2)}) %collective-permute-start.6) | collective-permute-done | bytes 262176 | tf_op jit(solution)/shard_map/ppermute | solution.py:36
  307.2 0.0 collective-permute-done.7
  307.2 1.1 fusion.12
  308.3 1.2 fusion.10
  309.5 1.2 subtract_select_fusion.2
  310.6 2.7 collective-permute-start.9
  313.3 3.4 collective-permute-start.8
  316.7 25.9 %collective-permute-done.8 = f32[256,256]{0,1:T(8,128)S(1)} collective-permute-done((f32[256,256]{0,1:T(8,128)S(1)}, f32[256,256]{0,1:T(8,128)S(1)}, u32[]{:S(2)}, u32[]{:S(2)}) %collective-permute-start.8) | collective-permute-done | bytes 262176 | tf_op jit(solution)/shard_map/ppermute | solution.py:36
  342.6 0.0 collective-permute-done.9
  342.6 1.1 fusion.7
  343.7 1.2 fusion.5
  344.9 1.2 subtract_select_fusion.1
  346.0 3.3 collective-permute-start.11
  349.4 4.0 %collective-permute-start.10 = (f32[256,256]{0,1:T(8,128)S(1)}, f32[256,256]{0,1:T(8,128)S(1)}, u32[]{:S(2)}, u32[]{:S(2)}) collective-permute-start(f32[256,256]{0,1:T(8,128)S(1)} %get-tuple-element.7), channel_id=1, source_target_pairs={{0,256},{8,264},{16,272},{24,280},{32,288},{40,296},{48,304},{56,3... | collective-permute-start | bytes 786440 | tf_op jit(solution)/shard_map/ppermute | solution.py:36
  353.4 25.2 %collective-permute-done.10 = f32[256,256]{0,1:T(8,128)S(1)} collective-permute-done((f32[256,256]{0,1:T(8,128)S(1)}, f32[256,256]{0,1:T(8,128)S(1)}, u32[]{:S(2)}, u32[]{:S(2)}) %collective-permute-start.10) | collective-permute-done | bytes 262176 | tf_op jit(solution)/shard_map/ppermute | solution.py:36
  378.6 0.0 collective-permute-done.11
  378.7 1.1 fusion.2
  379.7 1.2 fusion
  380.9 1.2 subtract_select_fusion
  382.1 1.5 pad_maximum_fusion
  (4 shorter events, 0.0 us)
Async XLA Ops:
  5.0 98.0 %copy-start.2 = (f32[512,1024]{1,0:T(8,128)S(1)}, f32[512,1024]{1,0:T(8,128)}, u32[]{:S(2)}) copy-start(f32[512,1024]{1,0:T(8,128)} %param.5) | copy-start | bytes 6291460
  5.0 98.0 %all-to-all-start = ((f32[8,32,3840]{2,1,0:T(8,128)}), f32[8,32,3840]{2,1,0:T(8,128)}, u32[]{:S(2)}, u32[]{:S(2)}) async-start(f32[8,32,3840]{2,1,0:T(8,128)} %stack.2), calls=%async_computation | async-start | bytes 7864320 | tf_op jit(solution)/shard_map/all_to_all | solution.py:15
  105.9 2.2 copy-start.3
  112.2 23.7 %collective-permute-start.1 = (f32[256,1024]{1,0:T(8,128)}, f32[256,1024]{1,0:T(8,128)}, u32[]{:S(2)}, u32[]{:S(2)}) collective-permute-start(f32[256,1024]{1,0:T(8,128)} %get-tuple-element.13), channel_id=1, source_target_pairs={{0,8},{8,0},{16,24},{24,16},{32,40},{40,32},{48,56},{56,48},{64,72... | collective-permute-start | bytes 3145736 | tf_op jit(solution)/shard_map/ppermute | solution.py:36
  130.0 5.8 %copy-start = (f32[256,6,256]{2,0,1:T(8,128)S(1)}, f32[256,6,256]{2,0,1:T(8,128)}, u32[]{:S(2)}) copy-start(f32[256,6,256]{2,0,1:T(8,128)} %copy.16) | copy-start | bytes 4718596
  132.2 6.0 %copy-start.1 = (f32[256,6,256]{2,0,1:T(8,128)S(1)}, f32[256,6,256]{2,0,1:T(8,128)}, u32[]{:S(2)}) copy-start(f32[256,6,256]{2,0,1:T(8,128)} %copy.14) | copy-start | bytes 4718596
  132.2 3.7 collective-permute-start
  140.5 33.0 %collective-permute-start.3 = (f32[256,1024]{1,0:T(8,128)S(1)}, f32[256,1024]{1,0:T(8,128)S(1)}, u32[]{:S(2)}, u32[]{:S(2)}) collective-permute-start(f32[256,1024]{1,0:T(8,128)S(1)} %subtract_select_fusion.5), channel_id=1, source_target_pairs={{0,16},{8,24},{16,0},{24,8},{32,48},{40,56},{48,32},{56,40},{64,80... | collective-permute-start | bytes 3145736 | tf_op jit(solution)/shard_map/ppermute | solution.py:36
  142.5 31.0 %collective-permute-start.2 = (f32[256,256]{0,1:T(8,128)S(1)}, f32[256,256]{0,1:T(8,128)S(1)}, u32[]{:S(2)}, u32[]{:S(2)}) collective-permute-start(f32[256,256]{0,1:T(8,128)S(1)} %get-tuple-element.11), channel_id=1, source_target_pairs={{0,16},{8,24},{16,0},{24,8},{32,48},{40,56},{48,32},{56,40},{64,80... | collective-permute-start | bytes 786440 | tf_op jit(solution)/shard_map/ppermute | solution.py:36
  176.9 61.1 %collective-permute-start.5 = (f32[256,1024]{1,0:T(8,128)S(1)}, f32[256,1024]{1,0:T(8,128)S(1)}, u32[]{:S(2)}, u32[]{:S(2)}) collective-permute-start(f32[256,1024]{1,0:T(8,128)S(1)} %subtract_select_fusion.4), channel_id=1, source_target_pairs={{0,32},{8,40},{16,48},{24,56},{32,0},{40,8},{48,16},{56,24},{64,96... | collective-permute-start | bytes 3145736 | tf_op jit(solution)/shard_map/ppermute | solution.py:36
  178.9 59.2 %collective-permute-start.4 = (f32[256,256]{0,1:T(8,128)S(1)}, f32[256,256]{0,1:T(8,128)S(1)}, u32[]{:S(2)}, u32[]{:S(2)}) collective-permute-start(f32[256,256]{0,1:T(8,128)S(1)} %get-tuple-element.10), channel_id=1, source_target_pairs={{0,32},{8,40},{16,48},{24,56},{32,0},{40,8},{48,16},{56,24},{64,96... | collective-permute-start | bytes 786440 | tf_op jit(solution)/shard_map/ppermute | solution.py:36
  241.5 65.7 %collective-permute-start.7 = (f32[256,1024]{1,0:T(8,128)S(1)}, f32[256,1024]{1,0:T(8,128)S(1)}, u32[]{:S(2)}, u32[]{:S(2)}) collective-permute-start(f32[256,1024]{1,0:T(8,128)S(1)} %subtract_select_fusion.3), channel_id=1, source_target_pairs={{0,64},{8,72},{16,80},{24,88},{32,96},{40,104},{48,112},{56,120},{... | collective-permute-start | bytes 3145736 | tf_op jit(solution)/shard_map/ppermute | solution.py:36
  249.7 57.5 %collective-permute-start.6 = (f32[256,256]{0,1:T(8,128)S(1)}, f32[256,256]{0,1:T(8,128)S(1)}, u32[]{:S(2)}, u32[]{:S(2)}) collective-permute-start(f32[256,256]{0,1:T(8,128)S(1)} %get-tuple-element.9), channel_id=1, source_target_pairs={{0,64},{8,72},{16,80},{24,88},{32,96},{40,104},{48,112},{56,120},{... | collective-permute-start | bytes 786440 | tf_op jit(solution)/shard_map/ppermute | solution.py:36
  310.6 32.0 %collective-permute-start.9 = (f32[256,1024]{1,0:T(8,128)S(1)}, f32[256,1024]{1,0:T(8,128)S(1)}, u32[]{:S(2)}, u32[]{:S(2)}) collective-permute-start(f32[256,1024]{1,0:T(8,128)S(1)} %subtract_select_fusion.2), channel_id=1, source_target_pairs={{0,128},{8,136},{16,144},{24,152},{32,160},{40,168},{48,176},{56,1... | collective-permute-start | bytes 3145736 | tf_op jit(solution)/shard_map/ppermute | solution.py:36
  313.3 29.3 %collective-permute-start.8 = (f32[256,256]{0,1:T(8,128)S(1)}, f32[256,256]{0,1:T(8,128)S(1)}, u32[]{:S(2)}, u32[]{:S(2)}) collective-permute-start(f32[256,256]{0,1:T(8,128)S(1)} %get-tuple-element.8), channel_id=1, source_target_pairs={{0,128},{8,136},{16,144},{24,152},{32,160},{40,168},{48,176},{56,1... | collective-permute-start | bytes 786440 | tf_op jit(solution)/shard_map/ppermute | solution.py:36
  346.0 32.6 %collective-permute-start.11 = (f32[256,1024]{1,0:T(8,128)S(1)}, f32[256,1024]{1,0:T(8,128)S(1)}, u32[]{:S(2)}, u32[]{:S(2)}) collective-permute-start(f32[256,1024]{1,0:T(8,128)S(1)} %subtract_select_fusion.1), channel_id=1, source_target_pairs={{0,256},{8,264},{16,272},{24,280},{32,288},{40,296},{48,304},{56,3... | collective-permute-start | bytes 3145736 | tf_op jit(solution)/shard_map/ppermute | solution.py:36
  349.4 29.3 %collective-permute-start.10 = (f32[256,256]{0,1:T(8,128)S(1)}, f32[256,256]{0,1:T(8,128)S(1)}, u32[]{:S(2)}, u32[]{:S(2)}) collective-permute-start(f32[256,256]{0,1:T(8,128)S(1)} %get-tuple-element.7), channel_id=1, source_target_pairs={{0,256},{8,264},{16,272},{24,280},{32,288},{40,296},{48,304},{56,3... | collective-permute-start | bytes 786440 | tf_op jit(solution)/shard_map/ppermute | solution.py:36
